TPU v7x, 32 devices: a whole 2x2x4 slice. The times are simulated.
32 devices in a mesh: grp: 4 (over z), brick: 8 (over y, x, core).
Axes of the slice: x: 2, y: 2, z: 4, core: 2. Of those that a mesh axis runs over, the one named last changes fastest.
Arguments:
- store: bfloat16 [96, 256, 256], P(('grp', 'brick')), may hold values from -0.01171875 to 0.01171875
- crossing: int32 [32, 4], P('grp'), may hold values from 0 to 23, as said below
- phi: bfloat16 [32, 64, 16, 1024], P('grp', 'brick'), may hold values from -6 to 6
- rows_index: int32 [32, 4, 256], P(('grp', 'brick')), may hold values from 0 to 1023
- cols_index: int32 [32, 4, 256], P(('grp', 'brick')), may hold values from 0 to 1023
Outputs:
- hamiltonian: float32 [96, 256, 256], P(('grp', 'brick'))
Inputs may be any that keep to these rules, and one draw needn't show every extreme that they name: `crossing`: each row lists 4 different blocks of its group; block k of a group is held by the device with brick index k // 3 of that group. A row names at most 1 block held by one device, and exactly 1 of some device.
All inputs are finite; a program needn't handle non-finite values.
Results may differ from a plain program's by a relative error of at most 0.0029.
Values may be sent and summed in bfloat16 or wider, within the bound.
A program may use at most 128 MiB of HBM per device.

v0:
```python
import math

import jax
import jax.numpy as jnp
from jax import lax
from jax.sharding import PartitionSpec as P

CAP = 1


GRAD_WEIGHT = 0.5


def extended(block, sides, width):
    for axis, dim in sides:
        count = lax.axis_size(axis)
        forward = [(i, i + 1) for i in range(count - 1)]
        forward.append((count - 1, 0))
        backward = [(target, source) for source, target in forward]
        low = lax.ppermute(
            lax.slice_in_dim(block, block.shape[dim] - width, None, axis=dim), axis, forward
        )
        high = lax.ppermute(lax.slice_in_dim(block, 0, width, axis=dim), axis, backward)
        block = jnp.concatenate([low, block, high], axis=dim)
    return block


def owner_rank(owners):
    count = owners.shape[-1]
    same_owner = owners[..., :, None] == owners[..., None, :]
    before = jnp.arange(count)[None, :] < jnp.arange(count)[:, None]
    return jnp.sum(same_owner & before, axis=-1)


def flux_of(padded):
    centre = padded[1:-1, 1:-1]
    grad_x = (padded[2:, 1:-1] - padded[:-2, 1:-1]) * 0.5
    grad_y = (padded[1:-1, 2:] - padded[1:-1, :-2]) * 0.5
    grad_z = (jnp.roll(centre, -1, 2) - jnp.roll(centre, 1, 2)) * 0.5
    sigma = grad_x * grad_x + grad_y * grad_y + grad_z * grad_z
    factor = 2.0 * GRAD_WEIGHT / (1.0 + sigma)
    return (factor * grad_x, factor * grad_y, factor * grad_z)


def along_z(field):
    return (jnp.roll(field, -1, 2) - jnp.roll(field, 1, 2)) * 0.5


def local(store, crossing, phi, rows_index, cols_index):
    brick_count = lax.axis_size("brick")
    position = lax.axis_index("brick")
    own_count = store.shape[0]
    width = store.shape[1]
    owners = crossing // own_count
    local_ids = crossing % own_count
    ranks = owner_rank(owners)
    slot_iota = jnp.arange(CAP, dtype=jnp.int32)
    chosen = (owners == position)[:, None, :] & (ranks[:, None, :] == slot_iota[None, :, None])
    filled = jnp.any(chosen, axis=-1)
    send_ids = jnp.sum(jnp.where(chosen, local_ids[:, None, :], 0), axis=-1)
    my_row = lax.dynamic_index_in_dim(crossing, position, 0, keepdims=False)
    my_owner = my_row // own_count
    my_slot = my_owner * CAP + owner_rank(my_owner)
    outgoing = jnp.where(filled[:, :, None, None], store[send_ids], jnp.zeros((), store.dtype))
    incoming = lax.all_to_all(outgoing, "brick", split_axis=0, concat_axis=0, tiled=True)
    blocks = incoming.reshape(brick_count * CAP, width, width)[my_slot]
    size_x, size_y, size_z = (phi.shape[0], phi.shape[1], phi.shape[2])
    points = size_x * size_y * size_z
    table = phi.reshape(points, phi.shape[3]).T
    row_tables = table[rows_index[0]]
    col_tables = table[cols_index[0]]

    def collocate(operands):
        block, left, right = operands
        product = jnp.dot(block, right, preferred_element_type=jnp.float32)
        return jnp.sum(left.astype(jnp.float32) * product, axis=0)

    density = jnp.sum(lax.map(collocate, (blocks, row_tables, col_tables)), axis=0).reshape(
        size_x, size_y, size_z
    )
    padded = extended(density, (("grp", 0), ("brick", 1)), 1)
    flux_x, flux_y, flux_z = flux_of(padded)
    stacked = jnp.stack([flux_x, flux_y])
    outer = extended(stacked, (("grp", 1), ("brick", 2)), 1)
    diverge = (
        (outer[0, 2:, 1:-1] - outer[0, :-2, 1:-1]) * 0.5
        + (outer[1, 1:-1, 2:] - outer[1, 1:-1, :-2]) * 0.5
        + along_z(flux_z)
    )
    potential = density / jnp.sqrt(1.0 + density * density) - diverge
    scaled = potential.reshape(points) * (1.0 / math.sqrt(points))

    def integrate(operands):
        left, right = operands
        weighted = (right.astype(jnp.float32) * scaled[None, :]).astype(jnp.bfloat16)
        return lax.dot_general(
            left, weighted, (((1,), (1,)), ((), ())), preferred_element_type=jnp.float32
        )

    partial_value = lax.map(integrate, (row_tables, col_tables))
    returning = (
        jnp.zeros((brick_count * CAP, width, width), jnp.float32).at[my_slot].set(partial_value)
    )
    returning = returning.reshape(brick_count, CAP, width, width)
    arrived = lax.all_to_all(returning, "brick", split_axis=0, concat_axis=0, tiled=True)
    onehot = (
        filled[:, :, None]
        & (send_ids[:, :, None] == jnp.arange(own_count, dtype=jnp.int32)[None, None, :])
    ).astype(jnp.float32)
    return jnp.einsum("dck,dcab->kab", onehot, arrived, precision=lax.Precision.HIGHEST)


def solution(mesh):
    in_specs = (
        P(("grp", "brick"), None, None),
        P("grp", None),
        P("grp", "brick", None, None),
        P(("grp", "brick"), None, None),
        P(("grp", "brick"), None, None),
    )
    out_specs = P(("grp", "brick"), None, None)
    return jax.shard_map(local, mesh=mesh, in_specs=in_specs, out_specs=out_specs, check_vma=False)
```

profile of v0, /device:TPU:1, one launch (start us, length us, event | category | flops | bytes accessed | tf_op | source)
XLA Modules:
  0.0 100.2 jit_solution(331570811692277714)
XLA Ops:
  4.8 5.2 %all-to-all-start = ((bf16[8,1,256,256]{3,2,1,0:T(8,128)(2,1)}), bf16[8,1,256,256]{3,2,1,0:T(8,128)(2,1)S(1)}, u32[]{:S(2)}, u32[]{:S(2)}) async-start(bf16[8,1,256,256]{3,2,1,0:T(8,128)(2,1)} %bitcast_select_fusion), calls=%async_computation | async-start | bytes 2097152 | tf_op jit(solution)/shard_map/all_to_all | solution.py:65
  10.0 2.9 %copy.22 = bf16[1024,1024]{0,1:T(8,128)(2,1)S(1)} copy(bf16[1024,1024]{1,0:T(8,128)(2,1)} %bitcast.96) | data formatting | bytes 4194304 | tf_op jit(solution)/shard_map/reshape | solution.py:69
  12.9 5.4 %gather_fusion.1 = bf16[1024,1024]{1,0:T(8,128)(2,1)} fusion(bf16[1024,1024]{1,0:T(8,128)(2,1)S(1)} %bitcast.90, s32[1024]{0:T(1024)S(1)} %get-tuple-element.108), kind=kCustom, calls=%fused_computation.1 | custom fusion | bytes 4198400 | tf_op jit(solution)/shard_map/gather | solution.py:71
  18.3 5.3 %gather_fusion = bf16[1024,1024]{1,0:T(8,128)(2,1)} fusion(bf16[1024,1024]{1,0:T(8,128)(2,1)S(1)} %bitcast.91, s32[1024]{0:T(1024)S(1)} %broadcast_clamp_fusion.1), kind=kCustom, calls=%fused_computation | custom fusion | bytes 4198400 | tf_op jit(solution)/shard_map/gather | solution.py:70
  24.9 11.6 %while.20 = (s32[]{:T(128)}, f32[4,1024]{1,0:T(4,128)}, bf16[4,256,1024]{2,1,0:T(8,128)(2,1)}, bf16[4,256,256]{2,1,0:T(8,128)(2,1)S(1)}, bf16[4,256,1024]{2,1,0:T(8,128)(2,1)}, /*index=5*/s32[]{:T(128)}, s32[]{:T(128)}) while((s32[]{:T(128)}, f32[4,1024]{1,0:T(4,128)}, bf16[4,256,1024]{2,1,0:T(8,128)(2,1)}, ...), condition=%wide.region_6.7_spmd, body=%wide.region_4.6_spmd.sunk | while | flops 135003136 | bytes 1193553 | solution.py:78
  24.9 1.6 %fusion.59 = f32[1024]{0:T(1024)S(1)} fusion(bf16[4,256,1024]{2,1,0:T(8,128)(2,1)} %get-tuple-element.189, s32[]{:T(128)} %get-tuple-element.178, bf16[4,256,1024]{2,1,0:T(8,128)(2,1)} %get-tuple-element.187, bf16[4,256,256]{2,1,0:T(8,128)(2,1)S(1)} %get-tuple-element.188), kind=kOutput, calls=%fused_computation.6.clone.1 | convolution fusion | flops 135003136 | bytes 1185280 | tf_op jit(solution)/shard_map/while/body/eval_jaxpr/dot_general | solution.py:75
  26.5 1.4 %dynamic_update_slice.11 = f32[4,1024]{1,0:T(4,128)} dynamic-update-slice(f32[4,1024]{1,0:T(4,128)} %get-tuple-element.179, f32[1,1024]{1,0:T(1,128)S(1)} %bitcast.97, s32[]{:T(128)} %get-tuple-element.178, s32[]{:T(128)} %constant.42.clone.1..sunk) | dynamic-update-slice | bytes 8196 | tf_op jit(solution)/shard_map/while/body/jit(dynamic_update_index_in_dim)/dynamic_update_slice | solution.py:78
  27.8 1.5 %fusion.59 = f32[1024]{0:T(1024)S(1)} fusion(bf16[4,256,1024]{2,1,0:T(8,128)(2,1)} %get-tuple-element.189, s32[]{:T(128)} %get-tuple-element.178, bf16[4,256,1024]{2,1,0:T(8,128)(2,1)} %get-tuple-element.187, bf16[4,256,256]{2,1,0:T(8,128)(2,1)S(1)} %get-tuple-element.188), kind=kOutput, calls=%fused_computation.6.clone.1 | convolution fusion | flops 135003136 | bytes 1185280 | tf_op jit(solution)/shard_map/while/body/eval_jaxpr/dot_general | solution.py:75
  29.3 1.4 %dynamic_update_slice.11 = f32[4,1024]{1,0:T(4,128)} dynamic-update-slice(f32[4,1024]{1,0:T(4,128)} %get-tuple-element.179, f32[1,1024]{1,0:T(1,128)S(1)} %bitcast.97, s32[]{:T(128)} %get-tuple-element.178, s32[]{:T(128)} %constant.42.clone.1..sunk) | dynamic-update-slice | bytes 8196 | tf_op jit(solution)/shard_map/while/body/jit(dynamic_update_index_in_dim)/dynamic_update_slice | solution.py:78
  30.7 1.5 %fusion.59 = f32[1024]{0:T(1024)S(1)} fusion(bf16[4,256,1024]{2,1,0:T(8,128)(2,1)} %get-tuple-element.189, s32[]{:T(128)} %get-tuple-element.178, bf16[4,256,1024]{2,1,0:T(8,128)(2,1)} %get-tuple-element.187, bf16[4,256,256]{2,1,0:T(8,128)(2,1)S(1)} %get-tuple-element.188), kind=kOutput, calls=%fused_computation.6.clone.1 | convolution fusion | flops 135003136 | bytes 1185280 | tf_op jit(solution)/shard_map/while/body/eval_jaxpr/dot_general | solution.py:75
  32.2 1.4 %dynamic_update_slice.11 = f32[4,1024]{1,0:T(4,128)} dynamic-update-slice(f32[4,1024]{1,0:T(4,128)} %get-tuple-element.179, f32[1,1024]{1,0:T(1,128)S(1)} %bitcast.97, s32[]{:T(128)} %get-tuple-element.178, s32[]{:T(128)} %constant.42.clone.1..sunk) | dynamic-update-slice | bytes 8196 | tf_op jit(solution)/shard_map/while/body/jit(dynamic_update_index_in_dim)/dynamic_update_slice | solution.py:78
  33.6 1.5 %fusion.59 = f32[1024]{0:T(1024)S(1)} fusion(bf16[4,256,1024]{2,1,0:T(8,128)(2,1)} %get-tuple-element.189, s32[]{:T(128)} %get-tuple-element.178, bf16[4,256,1024]{2,1,0:T(8,128)(2,1)} %get-tuple-element.187, bf16[4,256,256]{2,1,0:T(8,128)(2,1)S(1)} %get-tuple-element.188), kind=kOutput, calls=%fused_computation.6.clone.1 | convolution fusion | flops 135003136 | bytes 1185280 | tf_op jit(solution)/shard_map/while/body/eval_jaxpr/dot_general | solution.py:75
  38.7 2.0 %collective-permute-start = (f32[1,8,16]{2,1,0:T(8,128)S(1)}, f32[1,8,16]{2,1,0:T(8,128)S(1)}, u32[]{:S(2)}, u32[]{:S(2)}) collective-permute-start(f32[1,8,16]{2,1,0:T(8,128)S(1)} %slice.107), channel_id=1, source_target_pairs={{8,0},{16,8},{24,16},{0,24},{9,1},{17,9},{25,17},{1,25},{10,2},{18... | collective-permute-start | bytes 1544 | tf_op jit(solution)/shard_map/ppermute | solution.py:23
  41.7 2.3 %collective-permute-start.2 = (f32[10,1,16]{2,1,0:T(1,128)S(1)}, f32[10,1,16]{2,1,0:T(1,128)S(1)}, u32[]{:S(2)}, u32[]{:S(2)}) collective-permute-start(f32[10,1,16]{2,1,0:T(1,128)S(1)} %get-tuple-element.93), channel_id=1, source_target_pairs={{1,0},{2,1},{3,2},{4,3},{5,4},{6,5},{7,6},{0,7},{9,8},{10,9},{11,1... | collective-permute-start | bytes 1928 | tf_op jit(solution)/shard_map/ppermute | solution.py:23
  46.0 3.7 %collective-permute-start.4 = (f32[2,1,8,16]{3,2,1,0:T(8,128)S(1)}, f32[2,1,8,16]{3,2,1,0:T(8,128)S(1)}, u32[]{:S(2)}, u32[]{:S(2)}) collective-permute-start(f32[2,1,8,16]{3,2,1,0:T(8,128)S(1)} %get-tuple-element.92), channel_id=1, source_target_pairs={{8,0},{16,8},{24,16},{0,24},{9,1},{17,9},{25,17},{1,25},{10,2},{18... | collective-permute-start | bytes 3080 | tf_op jit(solution)/shard_map/ppermute | solution.py:23
  50.5 3.5 %collective-permute-done.5 = f32[2,1,8,16]{3,2,1,0:T(8,128)S(1)} collective-permute-done((f32[2,1,8,16]{3,2,1,0:T(8,128)S(1)}, f32[2,1,8,16]{3,2,1,0:T(8,128)S(1)}, u32[]{:S(2)}, u32[]{:S(2)}) %collective-permute-start.5) | collective-permute-done | bytes 1056 | tf_op jit(solution)/shard_map/ppermute | solution.py:20
  54.0 3.8 %collective-permute-start.6 = (f32[2,10,1,16]{3,2,1,0:T(1,128)S(1)}, f32[2,10,1,16]{3,2,1,0:T(1,128)S(1)}, u32[]{:S(2)}, u32[]{:S(2)}) collective-permute-start(f32[2,10,1,16]{3,2,1,0:T(1,128)S(1)} %get-tuple-element.89), channel_id=1, source_target_pairs={{1,0},{2,1},{3,2},{4,3},{5,4},{6,5},{7,6},{0,7},{9,8},{10,9},{11,1... | collective-permute-start | bytes 3848 | tf_op jit(solution)/shard_map/ppermute | solution.py:23
  59.1 6.3 %while.21 = (s32[]{:T(128)}, f32[4,256,256]{2,1,0:T(8,128)S(1)}, bf16[4,256,1024]{2,1,0:T(8,128)(2,1)}, bf16[4,256,1024]{2,1,0:T(8,128)(2,1)}, f32[1024]{0:T(1024)S(1)}, /*index=5*/s32[]{:T(128)}) while((s32[]{:T(128)}, f32[4,256,256]{2,1,0:T(8,128)S(1)}, bf16[4,256,1024]{2,1,0:T(8,128)(2,1)}, bf16[4,256,1024]{2,1,0:T(8,128)(2,1)}, ...), condition=%wide.region_9.10_spmd, body=%wide.region_8.9_spmd.sunk | while | flops 135004160 | bytes 1316421 | solution.py:100
  59.1 1.5 %fusion.62 = f32[4,256,256]{2,1,0:T(8,128)S(1)} fusion(f32[4,256,256]{2,1,0:T(8,128)S(1)} %get-tuple-element.199, s32[]{:T(128)} %get-tuple-element.198, f32[1024]{0:T(1024)S(1)} %get-tuple-element.208, bf16[4,256,1024]{2,1,0:T(8,128)(2,1)} %get-tuple-element.207, bf16[4,256,1024]{2,1,0:T(8,128)(2,1)} %get-tuple-element.206), kind=kOutput, calls=%fused_computation.13.clone.1 | convolution fusion | flops 135004160 | bytes 1316352 | tf_op jit(solution)/shard_map/while/body/eval_jaxpr/dot_general | solution.py:96
  60.7 1.5 %fusion.62 = f32[4,256,256]{2,1,0:T(8,128)S(1)} fusion(f32[4,256,256]{2,1,0:T(8,128)S(1)} %get-tuple-element.199, s32[]{:T(128)} %get-tuple-element.198, f32[1024]{0:T(1024)S(1)} %get-tuple-element.208, bf16[4,256,1024]{2,1,0:T(8,128)(2,1)} %get-tuple-element.207, bf16[4,256,1024]{2,1,0:T(8,128)(2,1)} %get-tuple-element.206), kind=kOutput, calls=%fused_computation.13.clone.1 | convolution fusion | flops 135004160 | bytes 1316352 | tf_op jit(solution)/shard_map/while/body/eval_jaxpr/dot_general | solution.py:96
  62.2 1.5 %fusion.62 = f32[4,256,256]{2,1,0:T(8,128)S(1)} fusion(f32[4,256,256]{2,1,0:T(8,128)S(1)} %get-tuple-element.199, s32[]{:T(128)} %get-tuple-element.198, f32[1024]{0:T(1024)S(1)} %get-tuple-element.208, bf16[4,256,1024]{2,1,0:T(8,128)(2,1)} %get-tuple-element.207, bf16[4,256,1024]{2,1,0:T(8,128)(2,1)} %get-tuple-element.206), kind=kOutput, calls=%fused_computation.13.clone.1 | convolution fusion | flops 135004160 | bytes 1316352 | tf_op jit(solution)/shard_map/while/body/eval_jaxpr/dot_general | solution.py:96
  63.8 1.5 %fusion.62 = f32[4,256,256]{2,1,0:T(8,128)S(1)} fusion(f32[4,256,256]{2,1,0:T(8,128)S(1)} %get-tuple-element.199, s32[]{:T(128)} %get-tuple-element.198, f32[1024]{0:T(1024)S(1)} %get-tuple-element.208, bf16[4,256,1024]{2,1,0:T(8,128)(2,1)} %get-tuple-element.207, bf16[4,256,1024]{2,1,0:T(8,128)(2,1)} %get-tuple-element.206), kind=kOutput, calls=%fused_computation.13.clone.1 | convolution fusion | flops 135004160 | bytes 1316352 | tf_op jit(solution)/shard_map/while/body/eval_jaxpr/dot_general | solution.py:96
  66.3 30.7 %all_to_all.10 = f32[8,1,256,256]{3,2,1,0:T(8,128)S(1)} all-to-all(f32[8,1,256,256]{3,2,1,0:T(8,128)S(1)} %bitcast.92), channel_id=1, replica_groups=mesh['grp'=4,'brick'=8] {'brick'}, dimensions={0} | all-to-all | bytes 4194304 | tf_op jit(solution)/shard_map/all_to_all | solution.py:105
  97.0 2.2 %fusion.14 = f32[3,256,256]{2,0,1:T(4,128)S(1)} fusion(f32[8,1,256,256]{3,2,1,0:T(8,128)S(1)} %all_to_all.10, s32[8]{0:T(128)S(1)} %fusion.28, pred[8]{0:T(512)(128)(4,1)S(1)} %get-tuple-element.85), kind=kOutput, calls=%fused_computation.21 | convolution fusion | flops 18874416 | bytes 2883624 | tf_op jit(solution)/shard_map/dck,dcab->kab/dot_general | solution.py:110
  (69 shorter events, 16.6 us)
Async XLA Ops:
  0.0 3.0 %copy-start = (bf16[3,256,256]{2,1,0:T(8,128)(2,1)S(1)}, bf16[3,256,256]{2,1,0:T(8,128)(2,1)}, u32[]{:S(2)}) copy-start(bf16[3,256,256]{2,1,0:T(8,128)(2,1)} %param.9) | copy-start | bytes 1179652
  3.6 6.4 %copy-start.3 = (s32[1,4,256]{2,1,0:T(4,128)S(1)}, s32[1,4,256]{2,1,0:T(4,128)}, u32[]{:S(2)}) copy-start(s32[1,4,256]{2,1,0:T(4,128)} %param.12) | copy-start | bytes 12292
  4.8 19.5 %all-to-all-start = ((bf16[8,1,256,256]{3,2,1,0:T(8,128)(2,1)}), bf16[8,1,256,256]{3,2,1,0:T(8,128)(2,1)S(1)}, u32[]{:S(2)}, u32[]{:S(2)}) async-start(bf16[8,1,256,256]{3,2,1,0:T(8,128)(2,1)} %bitcast_select_fusion), calls=%async_computation | async-start | bytes 2097152 | tf_op jit(solution)/shard_map/all_to_all | solution.py:65
  18.3 5.3 %copy-start.2 = (s32[8,4]{0,1:T(4,128)S(1)}, s32[8,4]{0,1:T(4,128)}, u32[]{:S(2)}) copy-start(s32[8,4]{0,1:T(4,128)} %param.10) | copy-start | bytes 388
  24.8 34.2 %copy-start.1 = (f32[4,256,256]{2,1,0:T(8,128)S(1)}, f32[4,256,256]{2,1,0:T(8,128)}, u32[]{:S(2)}) copy-start(f32[4,256,256]{2,1,0:T(8,128)} %custom-call.10) | copy-start | bytes 3145732
  37.3 4.3 %collective-permute-start.1 = (f32[1,8,16]{2,1,0:T(8,128)S(1)}, f32[1,8,16]{2,1,0:T(8,128)S(1)}, u32[]{:S(2)}, u32[]{:S(2)}) collective-permute-start(f32[1,8,16]{2,1,0:T(8,128)S(1)} %slice.110), channel_id=1, source_target_pairs={{0,8},{8,16},{16,24},{24,0},{1,9},{9,17},{17,25},{25,1},{2,10},{10... | collective-permute-start | bytes 1544 | tf_op jit(solution)/shard_map/ppermute | solution.py:20
  38.7 3.0 %collective-permute-start = (f32[1,8,16]{2,1,0:T(8,128)S(1)}, f32[1,8,16]{2,1,0:T(8,128)S(1)}, u32[]{:S(2)}, u32[]{:S(2)}) collective-permute-start(f32[1,8,16]{2,1,0:T(8,128)S(1)} %slice.107), channel_id=1, source_target_pairs={{8,0},{16,8},{24,16},{0,24},{9,1},{17,9},{25,17},{1,25},{10,2},{18... | collective-permute-start | bytes 1544 | tf_op jit(solution)/shard_map/ppermute | solution.py:23
  41.7 4.1 %collective-permute-start.2 = (f32[10,1,16]{2,1,0:T(1,128)S(1)}, f32[10,1,16]{2,1,0:T(1,128)S(1)}, u32[]{:S(2)}, u32[]{:S(2)}) collective-permute-start(f32[10,1,16]{2,1,0:T(1,128)S(1)} %get-tuple-element.93), channel_id=1, source_target_pairs={{1,0},{2,1},{3,2},{4,3},{5,4},{6,5},{7,6},{0,7},{9,8},{10,9},{11,1... | collective-permute-start | bytes 1928 | tf_op jit(solution)/shard_map/ppermute | solution.py:23
  44.0 1.8 %collective-permute-start.3 = (f32[10,1,16]{2,1,0:T(1,128)S(1)}, f32[10,1,16]{2,1,0:T(1,128)S(1)}, u32[]{:S(2)}, u32[]{:S(2)}) collective-permute-start(f32[10,1,16]{2,1,0:T(1,128)S(1)} %get-tuple-element.94), channel_id=1, source_target_pairs={{0,1},{1,2},{2,3},{3,4},{4,5},{5,6},{6,7},{7,0},{8,9},{9,10},{10,1... | collective-permute-start | bytes 1928 | tf_op jit(solution)/shard_map/ppermute | solution.py:20
  46.0 4.4 %collective-permute-start.4 = (f32[2,1,8,16]{3,2,1,0:T(8,128)S(1)}, f32[2,1,8,16]{3,2,1,0:T(8,128)S(1)}, u32[]{:S(2)}, u32[]{:S(2)}) collective-permute-start(f32[2,1,8,16]{3,2,1,0:T(8,128)S(1)} %get-tuple-element.92), channel_id=1, source_target_pairs={{8,0},{16,8},{24,16},{0,24},{9,1},{17,9},{25,17},{1,25},{10,2},{18... | collective-permute-start | bytes 3080 | tf_op jit(solution)/shard_map/ppermute | solution.py:23
  49.7 4.3 %collective-permute-start.5 = (f32[2,1,8,16]{3,2,1,0:T(8,128)S(1)}, f32[2,1,8,16]{3,2,1,0:T(8,128)S(1)}, u32[]{:S(2)}, u32[]{:S(2)}) collective-permute-start(f32[2,1,8,16]{3,2,1,0:T(8,128)S(1)} %get-tuple-element.91), channel_id=1, source_target_pairs={{0,8},{8,16},{16,24},{24,0},{1,9},{9,17},{17,25},{25,1},{2,10},{10... | collective-permute-start | bytes 3080 | tf_op jit(solution)/shard_map/ppermute | solution.py:20
  54.0 4.6 %collective-permute-start.6 = (f32[2,10,1,16]{3,2,1,0:T(1,128)S(1)}, f32[2,10,1,16]{3,2,1,0:T(1,128)S(1)}, u32[]{:S(2)}, u32[]{:S(2)}) collective-permute-start(f32[2,10,1,16]{3,2,1,0:T(1,128)S(1)} %get-tuple-element.89), channel_id=1, source_target_pairs={{1,0},{2,1},{3,2},{4,3},{5,4},{6,5},{7,6},{0,7},{9,8},{10,9},{11,1... | collective-permute-start | bytes 3848 | tf_op jit(solution)/shard_map/ppermute | solution.py:23
  57.8 1.2 %collective-permute-start.7 = (f32[2,10,1,16]{3,2,1,0:T(1,128)S(1)}, f32[2,10,1,16]{3,2,1,0:T(1,128)S(1)}, u32[]{:S(2)}, u32[]{:S(2)}) collective-permute-start(f32[2,10,1,16]{3,2,1,0:T(1,128)S(1)} %get-tuple-element.90), channel_id=1, source_target_pairs={{0,1},{1,2},{2,3},{3,4},{4,5},{5,6},{6,7},{7,0},{8,9},{9,10},{10,1... | collective-permute-start | bytes 3848 | tf_op jit(solution)/shard_map/ppermute | solution.py:20
where the time goes:
time: 102 us; the launch traced here: 100 us
  blocking collectives  30.7 us (30%)
  local copies, waits for them, and re-layouts  22.9 us (22%)
  starting transfers between devices  18.8 us (18%)
  matrix products  14.5 us (14%)
  waiting for transfers between devices  7.23 us (7%)
  other arithmetic  5.73 us (6%)
    all_to_all x1, blocking collectives, local(): lax.all_to_all(returning, 'brick', split_axis=0, concat_axis=0, tiled=True)  30.7 us
    ppermute x4, starting transfers between devices, extended(): lax.ppermute(lax.slice_in_dim(block, 0, width, axis=dim), axis, backward)  11.7 us
    dot_general x4, matrix products, integrate(): lax.dot_general(left, weighted, (((1,), (1,)), ((), ())), preferred_eleme...  6.19 us
    dot_general x4, matrix products, collocate(): product = jnp.dot(block, right, preferred_element_type=jnp.float32)  6.13 us
    dynamic_update_slice x4, local copies, waits for them, and re-layouts, local(): lax.map(collocate, (blocks, row_tables, col_tables))  5.43 us
    gather x1, local copies, waits for them, and re-layouts, local(): col_tables = table[cols_index[0]]  5.39 us
    gather x1, local copies, waits for them, and re-layouts, local(): row_tables = table[rows_index[0]]  5.33 us
    all_to_all x1, starting transfers between devices, local(): lax.all_to_all(outgoing, 'brick', split_axis=0, concat_axis=0, tiled=True)  5.21 us
  transfers between devices with their start and end apart: 9, of which 6 were waited for; matrix products, arithmetic and copies ran while one was open for 15% of the time, Pallas kernels for 0%

commit v1 on v0

v1 whole, which is shorter than its diff:
```python
import functools
import math

import jax
import jax.numpy as jnp
from jax import lax
from jax.experimental import pallas as pl
from jax.experimental.pallas import tpu as pltpu
from jax.sharding import PartitionSpec as P

GRAD_WEIGHT = 0.5
MESH = pl.DeviceIdType.MESH
NT = (((1,), (1,)), ((), ()))


def kernel(
    groups, bricks, size_z,
    crossing_ref, rows_ref, cols_ref, store_hbm, phi_hbm, out_ref,
    store_v, phi_v, outgoing, incoming, row_t, col_t, dens, halo, part, back, landed,
    load_sem, send_sem, recv_sem, halo_send, halo_recv, back_send, back_recv,
):
    group = lax.axis_index("grp")
    brick = lax.axis_index("brick")
    own, width = store_v.shape[0], store_v.shape[1]
    blocks = crossing_ref.shape[1]
    points, functions = phi_v.shape
    tall, wide = dens.shape

    load_store = pltpu.make_async_copy(store_hbm, store_v, load_sem.at[0])
    load_phi = pltpu.make_async_copy(phi_hbm, phi_v, load_sem.at[1])
    load_store.start()
    load_phi.start()

    def member(offset):
        return lax.rem(brick + (offset % bricks), bricks)

    def place(dg, db):
        return (lax.rem(group + (dg % groups), groups), member(db))

    around = [(dg, db) for dg in (-1, 0, 1) for db in (-1, 0, 1) if (dg, db) != (0, 0)]
    reached = {(0, r) for r in range(1, bricks)}
    reached |= {(dg % groups, db % bricks) for dg, db in around}
    reached = sorted(reached)
    barrier = pltpu.get_barrier_semaphore()
    for dg, db in reached:
        pl.semaphore_signal(barrier, inc=1, device_id=place(dg, db), device_id_type=MESH)

    def sent_to(whom, owner):
        number, taken = jnp.int32(0), jnp.int32(0)
        for j in range(blocks):
            entry = crossing_ref[whom, j]
            hit = lax.div(entry, own) == owner
            number = jnp.where(hit, lax.rem(entry, own), number)
            taken = jnp.where(hit, 1, taken)
        return number, taken

    load_store.wait()
    for r in range(1, bricks):
        number, _ = sent_to(member(r), brick)
        outgoing[r] = store_v[number]
    number, _ = sent_to(brick, brick)
    incoming[0] = store_v[number]
    pl.semaphore_wait(barrier, len(reached))
    sends = []
    for r in range(1, bricks):
        copy = pltpu.make_async_remote_copy(
            src_ref=outgoing.at[r], dst_ref=incoming.at[r],
            send_sem=send_sem.at[r], recv_sem=recv_sem.at[r],
            device_id=(group, member(r)), device_id_type=MESH,
        )
        copy.start()
        sends.append(copy)

    load_phi.wait()
    lane = lax.broadcasted_iota(jnp.int32, (width, 128), 1)

    def pick(index_ref, table_ref, j):
        index = jnp.broadcast_to(index_ref[0, pl.ds(j, 1), :], (128, width)).T
        onehot = jnp.concatenate(
            [
                jnp.where(index == lane + k * 128, 1.0, 0.0).astype(jnp.bfloat16)
                for k in range(functions // 128)
            ],
            axis=1,
        )
        table_ref[j] = lax.dot_general(
            onehot, phi_v[...], NT, preferred_element_type=jnp.float32
        ).astype(jnp.bfloat16)

    def tabulate(j, carry):
        pick(rows_ref, row_t, j)
        pick(cols_ref, col_t, j)
        return carry

    lax.fori_loop(0, blocks, tabulate, 0)

    for copy in sends:
        copy.wait()

    def collocate(j, total):
        owner = lax.div(crossing_ref[brick, j], own)
        slot = lax.rem(brick - owner + bricks, bricks)
        product = jnp.dot(incoming[slot], col_t[j], preferred_element_type=jnp.float32)
        return total + jnp.sum(row_t[j].astype(jnp.float32) * product, axis=0, keepdims=True)

    density = lax.fori_loop(0, blocks, collocate, jnp.zeros((1, points), jnp.float32))
    for x in range(tall):
        dens[x : x + 1, :] = density[:, x * wide : (x + 1) * wide]
    halo[1, 1] = dens[...]
    exchange = []
    for n, (dg, db) in enumerate(around):
        copy = pltpu.make_async_remote_copy(
            src_ref=dens, dst_ref=halo.at[1 - dg, 1 - db],
            send_sem=halo_send.at[n], recv_sem=halo_recv.at[n],
            device_id=place(dg, db), device_id_type=MESH,
        )
        copy.start()
        exchange.append(copy)
    for copy in exchange:
        copy.wait()

    field = jnp.concatenate(
        [jnp.concatenate([halo[i, k] for k in range(3)], axis=1) for i in range(3)], axis=0
    )
    rows, lanes = field.shape
    depth = lax.rem(lax.broadcasted_iota(jnp.int32, field.shape, 1), size_z)

    def along_x(f):
        return (pltpu.roll(f, rows - 1, 0) - pltpu.roll(f, 1, 0)) * 0.5

    def along_y(f):
        return (pltpu.roll(f, lanes - size_z, 1) - pltpu.roll(f, size_z, 1)) * 0.5

    def along_z(f):
        up = jnp.where(
            depth == size_z - 1, pltpu.roll(f, size_z - 1, 1), pltpu.roll(f, lanes - 1, 1)
        )
        down = jnp.where(depth == 0, pltpu.roll(f, lanes - size_z + 1, 1), pltpu.roll(f, 1, 1))
        return (up - down) * 0.5

    grad_x, grad_y, grad_z = along_x(field), along_y(field), along_z(field)
    sigma = grad_x * grad_x + grad_y * grad_y + grad_z * grad_z
    factor = 2.0 * GRAD_WEIGHT / (1.0 + sigma)
    diverge = along_x(factor * grad_x) + along_y(factor * grad_y) + along_z(factor * grad_z)
    centre = field[tall : 2 * tall, wide : 2 * wide]
    potential = centre / jnp.sqrt(1.0 + centre * centre) - diverge[
        tall : 2 * tall, wide : 2 * wide
    ]
    scaled = potential * (1.0 / math.sqrt(points))
    scaled = jnp.concatenate([scaled[x : x + 1, :] for x in range(tall)], axis=1)

    def integrate(j, carry):
        weighted = (col_t[j].astype(jnp.float32) * scaled).astype(jnp.bfloat16)
        part[j] = lax.dot_general(
            row_t[j], weighted, NT, preferred_element_type=jnp.float32
        ).astype(jnp.bfloat16)
        return carry

    lax.fori_loop(0, blocks, integrate, 0)

    returns = []
    for r in range(1, bricks):
        owner = member(r)
        which = jnp.int32(0)
        for j in range(blocks):
            which = jnp.where(lax.div(crossing_ref[brick, j], own) == owner, j, which)
        back[r] = part[which]
        copy = pltpu.make_async_remote_copy(
            src_ref=back.at[r], dst_ref=landed.at[r],
            send_sem=back_send.at[r], recv_sem=back_recv.at[r],
            device_id=(group, owner), device_id_type=MESH,
        )
        copy.start()
        returns.append(copy)

    which = jnp.int32(0)
    for j in range(blocks):
        which = jnp.where(lax.div(crossing_ref[brick, j], own) == brick, j, which)
    number, taken = sent_to(brick, brick)
    value = part[which].astype(jnp.float32)
    for k in range(own):
        out_ref[k] = jnp.where((taken == 1) & (number == k), value, 0.0)
    for r in range(1, bricks):
        number, taken = sent_to(member(-r), brick)
        returns[r - 1].wait()
        value = landed[r].astype(jnp.float32)
        for k in range(own):
            out_ref[k] = out_ref[k] + jnp.where((taken == 1) & (number == k), value, 0.0)


def local(groups, bricks, store, crossing, phi, rows_index, cols_index):
    own, width = store.shape[0], store.shape[1]
    blocks = crossing.shape[1]
    size_x, size_y, size_z, functions = phi.shape
    points = size_x * size_y * size_z
    tall, wide = size_x, size_y * size_z
    slots = (bricks, width, width)
    return pl.pallas_call(
        functools.partial(kernel, groups, bricks, size_z),
        out_shape=jax.ShapeDtypeStruct((own, width, width), jnp.float32),
        in_specs=[
            pl.BlockSpec(memory_space=pltpu.SMEM),
            pl.BlockSpec(memory_space=pltpu.VMEM),
            pl.BlockSpec(memory_space=pltpu.VMEM),
            pl.BlockSpec(memory_space=pl.ANY),
            pl.BlockSpec(memory_space=pl.ANY),
        ],
        out_specs=pl.BlockSpec(memory_space=pltpu.VMEM),
        scratch_shapes=[
            pltpu.VMEM((own, width, width), jnp.bfloat16),
            pltpu.VMEM((points, functions), jnp.bfloat16),
            pltpu.VMEM(slots, jnp.bfloat16),
            pltpu.VMEM(slots, jnp.bfloat16),
            pltpu.VMEM((blocks, width, points), jnp.bfloat16),
            pltpu.VMEM((blocks, width, points), jnp.bfloat16),
            pltpu.VMEM((tall, wide), jnp.float32),
            pltpu.VMEM((3, 3, tall, wide), jnp.float32),
            pltpu.VMEM((blocks, width, width), jnp.bfloat16),
            pltpu.VMEM(slots, jnp.bfloat16),
            pltpu.VMEM(slots, jnp.bfloat16),
            pltpu.SemaphoreType.DMA((2,)),
            pltpu.SemaphoreType.DMA((bricks,)),
            pltpu.SemaphoreType.DMA((bricks,)),
            pltpu.SemaphoreType.DMA((8,)),
            pltpu.SemaphoreType.DMA((8,)),
            pltpu.SemaphoreType.DMA((bricks,)),
            pltpu.SemaphoreType.DMA((bricks,)),
        ],
        compiler_params=pltpu.CompilerParams(
            collective_id=0, has_side_effects=True, vmem_limit_bytes=60 << 20
        ),
    )(crossing, rows_index, cols_index, store, phi.reshape(points, functions))


def solution(mesh):
    in_specs = (
        P(("grp", "brick"), None, None),
        P("grp", None),
        P("grp", "brick", None, None),
        P(("grp", "brick"), None, None),
        P(("grp", "brick"), None, None),
    )
    out_specs = P(("grp", "brick"), None, None)
    body = functools.partial(local, mesh.shape["grp"], mesh.shape["brick"])
    return jax.shard_map(body, mesh=mesh, in_specs=in_specs, out_specs=out_specs, check_vma=False)
```

time: 102 us -> 43 us (0.42); the launches traced: 100 us -> 42.7 us
  Pallas kernels: 0 us -> 39.3 us
  blocking collectives: 30.7 us -> 0 us
  local copies, waits for them, and re-layouts: 22.9 us -> 3.41 us
  starting transfers between devices: 18.8 us -> 0 us
  matrix products: 14.5 us -> 0 us
  waiting for transfers between devices: 7.23 us -> 0 us
  other arithmetic: 5.73 us -> 0 us
    pallas_call x0 -> x1, Pallas kernels: none -> 39.3 us  [local(): pl.pallas_call(functools.partial(kernel, groups, bricks, size_z), out_sha...]
    all_to_all x1 -> x0, blocking collectives: 30.7 us -> none  [local(): lax.all_to_all(returning, 'brick', split_axis=0, concat_axis=0, tiled=True)]
    dot_general x9 -> x0, matrix products: 14.5 us -> none  [the longest x4 6.19 us: integrate(): lax.dot_general(left, weighted, (((1,), (1,)), ((), ())), preferred_eleme...]
    ppermute x8 -> x0, starting transfers between devices: 13.6 us -> none  [the longest x4 11.7 us: extended(): lax.ppermute(lax.slice_in_dim(block, 0, width, axis=dim), axis, backward)]
    gather x4 -> x0, local copies, waits for them, and re-layouts: 11.9 us -> none  [the longest x1 5.39 us: local(): col_tables = table[cols_index[0]]]
    ppermute x8 -> x0, waiting for transfers between devices: 7.23 us -> none  [the longest x4 4.64 us: extended(): lax.ppermute(lax.slice_in_dim(block, block.shape[dim] - width, None, axis...]
    dynamic_update_slice x4 -> x0, local copies, waits for them, and re-layouts: 5.43 us -> none  [local(): lax.map(collocate, (blocks, row_tables, col_tables))]
    all_to_all x1 -> x0, starting transfers between devices: 5.21 us -> none  [local(): lax.all_to_all(outgoing, 'brick', split_axis=0, concat_axis=0, tiled=True)]
  transfers between devices with their start and end apart: 9 -> 0, of which waited for: 6 -> 0; matrix products, arithmetic and copies ran while one was open for 15% -> 0% of each run, Pallas kernels for 0% -> 0%
where the time goes in v1:
time: 43 us; the launch traced here: 42.7 us
  Pallas kernels  39.3 us (91%)
  local copies, waits for them, and re-layouts  3.41 us (8%)
    pallas_call x1, Pallas kernels, local(): pl.pallas_call(functools.partial(kernel, groups, bricks, size_z), out_sha...  39.3 us
    unnamed x2, local copies, waits for them, and re-layouts  3.41 us

profile of v1, /device:TPU:1, one launch (start us, length us, event | category | flops | bytes accessed | tf_op | source)
XLA Modules:
  0.0 42.7 jit_solution(6320764810735696415)
XLA Ops:
  0.0 1.3 %copy.6.crossing_ref = s32[8,4]{1,0:T(8,128)} copy(s32[8,4]{0,1:T(4,128)} %param.6) | data formatting | bytes 256 | tf_op args[1]
  1.3 39.3 %shard_map.55 = f32[3,256,256]{2,1,0:T(8,128)} custom-call(s32[8,4]{1,0:T(8,128)} %copy.6.crossing_ref, s32[1,4,256]{2,1,0:T(4,128)} %rows_ref.1, s32[1,4,256]{2,1,0:T(4,128)} %cols_ref.1, bf16[3,256,256]{2,1,0:T(8,128)(2,1)} %store_hbm.1, bf16[1024,1024]{1,0:T(8,128)(2,1)} %bitcast.1), custom_call_target="tpu_custom_call" | custom-call | tf_op jit(solution)/shard_map/pallas_call | solution.py:198
  40.7 2.1 %copy.8 = f32[3,256,256]{2,1,0:T(8,128)} copy(f32[3,256,256]{2,1,0:T(8,128)} %shard_map.55) | data formatting | bytes 1572864

commit v2 on v1

--- a/solution.py
+++ b/solution.py
@@ -13,26 +13,53 @@
 NT = (((1,), (1,)), ((), ()))
 
 
+def partner_of(bricks, brick, r):
+    if bricks & (bricks - 1):
+        return lax.rem(r - brick + bricks, bricks)
+    other = brick
+    for bit in range(bricks.bit_length() - 1):
+        if r >> bit & 1:
+            other = other + (1 << bit) * (1 - 2 * lax.rem(lax.div(brick, 1 << bit), 2))
+    return other
+
+
+def block_number(crossing_ref, own, whom, owner):
+    number, taken = jnp.int32(0), jnp.int32(0)
+    for j in range(crossing_ref.shape[0]):
+        entry = crossing_ref[j, whom]
+        hit = lax.div(entry, own) == owner
+        number = jnp.where(hit, lax.rem(entry, own), number)
+        taken = jnp.where(hit, 1, taken)
+    return number, taken
+
+
 def kernel(
     groups, bricks, size_z,
-    crossing_ref, rows_ref, cols_ref, store_hbm, phi_hbm, out_ref,
-    store_v, phi_v, outgoing, incoming, row_t, col_t, dens, halo, part, back, landed,
+    crossing_ref, rows_hbm, cols_hbm, store_hbm, phi_hbm, landed,
+    rows_ref, cols_ref, store_v, phi_v, outgoing, incoming, row_t, col_t, dens, halo, back,
     load_sem, send_sem, recv_sem, halo_send, halo_recv, back_send, back_recv,
 ):
     group = lax.axis_index("grp")
     brick = lax.axis_index("brick")
     own, width = store_v.shape[0], store_v.shape[1]
-    blocks = crossing_ref.shape[1]
+    blocks = crossing_ref.shape[0]
     points, functions = phi_v.shape
     tall, wide = dens.shape
 
     load_store = pltpu.make_async_copy(store_hbm, store_v, load_sem.at[0])
     load_phi = pltpu.make_async_copy(phi_hbm, phi_v, load_sem.at[1])
+    load_rows = pltpu.make_async_copy(rows_hbm, rows_ref, load_sem.at[2])
+    load_cols = pltpu.make_async_copy(cols_hbm, cols_ref, load_sem.at[3])
     load_store.start()
     load_phi.start()
+    load_rows.start()
+    load_cols.start()
 
     def member(offset):
         return lax.rem(brick + (offset % bricks), bricks)
+
+    partner = functools.partial(partner_of, bricks, brick)
+    order = sorted(range(1, bricks), key=lambda r: (r == 1, r & 1, -bin(r >> 1).count("1")))
 
     def place(dg, db):
         return (lax.rem(group + (dg % groups), groups), member(db))
@@ -45,32 +72,33 @@
     for dg, db in reached:
         pl.semaphore_signal(barrier, inc=1, device_id=place(dg, db), device_id_type=MESH)
 
-    def sent_to(whom, owner):
-        number, taken = jnp.int32(0), jnp.int32(0)
+    def position_of(owner):
+        where, taken = jnp.int32(0), jnp.int32(0)
         for j in range(blocks):
-            entry = crossing_ref[whom, j]
-            hit = lax.div(entry, own) == owner
-            number = jnp.where(hit, lax.rem(entry, own), number)
+            hit = lax.div(crossing_ref[j, brick], own) == owner
+            where = jnp.where(hit, j, where)
             taken = jnp.where(hit, 1, taken)
-        return number, taken
+        return where, taken
 
     load_store.wait()
-    for r in range(1, bricks):
-        number, _ = sent_to(member(r), brick)
+    for r in order:
+        number, _ = block_number(crossing_ref, own, partner(r), brick)
         outgoing[r] = store_v[number]
-    number, _ = sent_to(brick, brick)
+    number, _ = block_number(crossing_ref, own, brick, brick)
     incoming[0] = store_v[number]
     pl.semaphore_wait(barrier, len(reached))
     sends = []
-    for r in range(1, bricks):
+    for r in order:
         copy = pltpu.make_async_remote_copy(
             src_ref=outgoing.at[r], dst_ref=incoming.at[r],
             send_sem=send_sem.at[r], recv_sem=recv_sem.at[r],
-            device_id=(group, member(r)), device_id_type=MESH,
+            device_id=(group, partner(r)), device_id_type=MESH,
         )
         copy.start()
         sends.append(copy)
 
+    load_rows.wait()
+    load_cols.wait()
     load_phi.wait()
     lane = lax.broadcasted_iota(jnp.int32, (width, 128), 1)
 
@@ -94,16 +122,14 @@
 
     lax.fori_loop(0, blocks, tabulate, 0)
 
-    for copy in sends:
-        copy.wait()
-
-    def collocate(j, total):
-        owner = lax.div(crossing_ref[brick, j], own)
-        slot = lax.rem(brick - owner + bricks, bricks)
-        product = jnp.dot(incoming[slot], col_t[j], preferred_element_type=jnp.float32)
-        return total + jnp.sum(row_t[j].astype(jnp.float32) * product, axis=0, keepdims=True)
-
-    density = lax.fori_loop(0, blocks, collocate, jnp.zeros((1, points), jnp.float32))
+    density = jnp.zeros((1, points), jnp.float32)
+    for n, r in enumerate([0] + order):
+        where, taken = position_of(partner(r) if r else brick)
+        if n:
+            sends[n - 1].wait()
+        product = jnp.dot(incoming[r], col_t[where], preferred_element_type=jnp.float32)
+        term = jnp.sum(row_t[where].astype(jnp.float32) * product, axis=0, keepdims=True)
+        density = density + jnp.where(taken == 1, term, 0.0)
     for x in range(tall):
         dens[x : x + 1, :] = density[:, x * wide : (x + 1) * wide]
     halo[1, 1] = dens[...]
@@ -149,64 +175,63 @@
     scaled = potential * (1.0 / math.sqrt(points))
     scaled = jnp.concatenate([scaled[x : x + 1, :] for x in range(tall)], axis=1)
 
-    def integrate(j, carry):
-        weighted = (col_t[j].astype(jnp.float32) * scaled).astype(jnp.bfloat16)
-        part[j] = lax.dot_general(
-            row_t[j], weighted, NT, preferred_element_type=jnp.float32
+    returns = []
+    for r in order + [0]:
+        where, _ = position_of(partner(r) if r else brick)
+        weighted = (col_t[where].astype(jnp.float32) * scaled).astype(jnp.bfloat16)
+        back[r] = lax.dot_general(
+            row_t[where], weighted, NT, preferred_element_type=jnp.float32
         ).astype(jnp.bfloat16)
-        return carry
-
-    lax.fori_loop(0, blocks, integrate, 0)
-
-    returns = []
-    for r in range(1, bricks):
-        owner = member(r)
-        which = jnp.int32(0)
-        for j in range(blocks):
-            which = jnp.where(lax.div(crossing_ref[brick, j], own) == owner, j, which)
-        back[r] = part[which]
-        copy = pltpu.make_async_remote_copy(
-            src_ref=back.at[r], dst_ref=landed.at[r],
-            send_sem=back_send.at[r], recv_sem=back_recv.at[r],
-            device_id=(group, owner), device_id_type=MESH,
-        )
+        if r:
+            copy = pltpu.make_async_remote_copy(
+                src_ref=back.at[r], dst_ref=landed.at[r],
+                send_sem=back_send.at[r], recv_sem=back_recv.at[r],
+                device_id=(group, partner(r)), device_id_type=MESH,
+            )
+        else:
+            copy = pltpu.make_async_copy(back.at[0], landed.at[0], load_sem.at[4])
         copy.start()
         returns.append(copy)
-
-    which = jnp.int32(0)
-    for j in range(blocks):
-        which = jnp.where(lax.div(crossing_ref[brick, j], own) == brick, j, which)
-    number, taken = sent_to(brick, brick)
-    value = part[which].astype(jnp.float32)
+    for copy in returns:
+        copy.wait()
+
+
+def gather_up(bricks, crossing_ref, landed_ref, out_ref):
+    brick = lax.axis_index("brick")
+    own = out_ref.shape[0]
+    totals = [jnp.zeros(out_ref.shape[1:], jnp.float32) for _ in range(own)]
+    for r in range(bricks):
+        whom = partner_of(bricks, brick, r) if r else brick
+        number, taken = block_number(crossing_ref, own, whom, brick)
+        value = landed_ref[r].astype(jnp.float32)
+        for k in range(own):
+            totals[k] = totals[k] + jnp.where((taken == 1) & (number == k), value, 0.0)
     for k in range(own):
-        out_ref[k] = jnp.where((taken == 1) & (number == k), value, 0.0)
-    for r in range(1, bricks):
-        number, taken = sent_to(member(-r), brick)
-        returns[r - 1].wait()
-        value = landed[r].astype(jnp.float32)
-        for k in range(own):
-            out_ref[k] = out_ref[k] + jnp.where((taken == 1) & (number == k), value, 0.0)
+        out_ref[k] = totals[k]
 
 
 def local(groups, bricks, store, crossing, phi, rows_index, cols_index):
     own, width = store.shape[0], store.shape[1]
-    blocks = crossing.shape[1]
+    crossing = crossing.T
+    blocks = crossing.shape[0]
     size_x, size_y, size_z, functions = phi.shape
     points = size_x * size_y * size_z
     tall, wide = size_x, size_y * size_z
     slots = (bricks, width, width)
-    return pl.pallas_call(
+    landed = pl.pallas_call(
         functools.partial(kernel, groups, bricks, size_z),
-        out_shape=jax.ShapeDtypeStruct((own, width, width), jnp.float32),
+        out_shape=jax.ShapeDtypeStruct(slots, jnp.bfloat16),
         in_specs=[
             pl.BlockSpec(memory_space=pltpu.SMEM),
-            pl.BlockSpec(memory_space=pltpu.VMEM),
-            pl.BlockSpec(memory_space=pltpu.VMEM),
+            pl.BlockSpec(memory_space=pl.ANY),
+            pl.BlockSpec(memory_space=pl.ANY),
             pl.BlockSpec(memory_space=pl.ANY),
             pl.BlockSpec(memory_space=pl.ANY),
         ],
-        out_specs=pl.BlockSpec(memory_space=pltpu.VMEM),
+        out_specs=pl.BlockSpec(memory_space=pl.ANY),
         scratch_shapes=[
+            pltpu.VMEM(rows_index.shape, jnp.int32),
+            pltpu.VMEM(cols_index.shape, jnp.int32),
             pltpu.VMEM((own, width, width), jnp.bfloat16),
             pltpu.VMEM((points, functions), jnp.bfloat16),
             pltpu.VMEM(slots, jnp.bfloat16),
@@ -215,10 +240,8 @@
             pltpu.VMEM((blocks, width, points), jnp.bfloat16),
             pltpu.VMEM((tall, wide), jnp.float32),
             pltpu.VMEM((3, 3, tall, wide), jnp.float32),
-            pltpu.VMEM((blocks, width, width), jnp.bfloat16),
             pltpu.VMEM(slots, jnp.bfloat16),
-            pltpu.VMEM(slots, jnp.bfloat16),
-            pltpu.SemaphoreType.DMA((2,)),
+            pltpu.SemaphoreType.DMA((5,)),
             pltpu.SemaphoreType.DMA((bricks,)),
             pltpu.SemaphoreType.DMA((bricks,)),
             pltpu.SemaphoreType.DMA((8,)),
@@ -230,6 +253,17 @@
             collective_id=0, has_side_effects=True, vmem_limit_bytes=60 << 20
         ),
     )(crossing, rows_index, cols_index, store, phi.reshape(points, functions))
+    strip = 64 if width % 64 == 0 else width
+    return pl.pallas_call(
+        functools.partial(gather_up, bricks),
+        out_shape=jax.ShapeDtypeStruct((own, width, width), jnp.float32),
+        grid=(width // strip,),
+        in_specs=[
+            pl.BlockSpec(memory_space=pltpu.SMEM),
+            pl.BlockSpec((bricks, strip, width), lambda i: (0, i, 0)),
+        ],
+        out_specs=pl.BlockSpec((own, strip, width), lambda i: (0, i, 0)),
+    )(crossing, landed)
 
 
 def solution(mesh):

time: 43 us -> 42.9 us (level)
  local copies, waits for them, and re-layouts: 3.41 us -> 0 us
  Pallas kernels: 39.3 us -> 42.3 us
    pallas_call x0 -> x1, Pallas kernels: none -> 3.84 us  [local(): pl.pallas_call(functools.partial(gather_up, bricks), out_shape=jax.ShapeD...]
    unnamed x2 -> x0, local copies, waits for them, and re-layouts: 3.41 us -> none
    pallas_call x1, Pallas kernels: 39.3 us -> 38.4 us  [local(): pl.pallas_call(functools.partial(kernel, groups, bricks, size_z), out_sha...]
where the time goes in v2:
time: 42.9 us; the launch traced here: 42.3 us
  Pallas kernels  42.3 us (99%)
    pallas_call x1, Pallas kernels, local(): pl.pallas_call(functools.partial(kernel, groups, bricks, size_z), out_sha...  38.4 us
    pallas_call x1, Pallas kernels, local(): pl.pallas_call(functools.partial(gather_up, bricks), out_shape=jax.ShapeD...  3.84 us

profile of v2, /device:TPU:1, one launch (start us, length us, event | category | flops | bytes accessed | tf_op | source)
XLA Modules:
  0.0 42.3 jit_solution(10418965437459074118)
XLA Ops:
  0.0 38.4 %shard_map.55.landed_ref = bf16[8,256,256]{2,1,0:T(8,128)(2,1)} custom-call(s32[4,8]{1,0:T(4,128)} %bitcast.3, s32[1,4,256]{2,1,0:T(4,128)} %rows_hbm.1, s32[1,4,256]{2,1,0:T(4,128)} %cols_hbm.1, bf16[3,256,256]{2,1,0:T(8,128)(2,1)} %store_hbm.1, bf16[1024,1024]{1,0:T(8,128)(2,1)} %bitcast.2), custom_call_target="tpu_custom_call" | custom-call | tf_op jit(solution)/shard_map/pallas_call | solution.py:221
  38.4 3.8 %shard_map.56 = f32[3,256,256]{2,1,0:T(8,128)} custom-call(s32[4,8]{1,0:T(4,128)} %bitcast.4, bf16[8,256,256]{2,1,0:T(8,128)(2,1)} %shard_map.55.landed_ref), custom_call_target="tpu_custom_call" | custom-call | tf_op jit(solution)/shard_map/pallas_call | solution.py:257

commit v3 on v2

--- a/solution.py
+++ b/solution.py
@@ -35,8 +35,8 @@
 
 def kernel(
     groups, bricks, size_z,
-    crossing_ref, rows_hbm, cols_hbm, store_hbm, phi_hbm, landed,
-    rows_ref, cols_ref, store_v, phi_v, outgoing, incoming, row_t, col_t, dens, halo, back,
+    crossing_ref, rows_hbm, cols_hbm, store_hbm, phi_hbm, out_ref,
+    rows_ref, cols_ref, store_v, phi_v, outgoing, incoming, row_t, col_t, dens, halo, back, landed,
     load_sem, send_sem, recv_sem, halo_send, halo_recv, back_send, back_recv,
 ):
     group = lax.axis_index("grp")
@@ -188,26 +188,16 @@
                 send_sem=back_send.at[r], recv_sem=back_recv.at[r],
                 device_id=(group, partner(r)), device_id_type=MESH,
             )
-        else:
-            copy = pltpu.make_async_copy(back.at[0], landed.at[0], load_sem.at[4])
-        copy.start()
-        returns.append(copy)
-    for copy in returns:
-        copy.wait()
-
-
-def gather_up(bricks, crossing_ref, landed_ref, out_ref):
-    brick = lax.axis_index("brick")
-    own = out_ref.shape[0]
-    totals = [jnp.zeros(out_ref.shape[1:], jnp.float32) for _ in range(own)]
-    for r in range(bricks):
-        whom = partner_of(bricks, brick, r) if r else brick
-        number, taken = block_number(crossing_ref, own, whom, brick)
-        value = landed_ref[r].astype(jnp.float32)
+            copy.start()
+            returns.append(copy)
+    for n, r in enumerate([0] + order):
+        number, taken = block_number(crossing_ref, own, partner(r) if r else brick, brick)
+        if n:
+            returns[n - 1].wait()
+        value = (landed if n else back)[r].astype(jnp.float32)
         for k in range(own):
-            totals[k] = totals[k] + jnp.where((taken == 1) & (number == k), value, 0.0)
-    for k in range(own):
-        out_ref[k] = totals[k]
+            term = jnp.where((taken == 1) & (number == k), value, 0.0)
+            out_ref[k] = out_ref[k] + term if n else term
 
 
 def local(groups, bricks, store, crossing, phi, rows_index, cols_index):
@@ -218,9 +208,9 @@
     points = size_x * size_y * size_z
     tall, wide = size_x, size_y * size_z
     slots = (bricks, width, width)
-    landed = pl.pallas_call(
+    return pl.pallas_call(
         functools.partial(kernel, groups, bricks, size_z),
-        out_shape=jax.ShapeDtypeStruct(slots, jnp.bfloat16),
+        out_shape=jax.ShapeDtypeStruct((own, width, width), jnp.float32),
         in_specs=[
             pl.BlockSpec(memory_space=pltpu.SMEM),
             pl.BlockSpec(memory_space=pl.ANY),
@@ -228,7 +218,7 @@
             pl.BlockSpec(memory_space=pl.ANY),
             pl.BlockSpec(memory_space=pl.ANY),
         ],
-        out_specs=pl.BlockSpec(memory_space=pl.ANY),
+        out_specs=pl.BlockSpec(memory_space=pltpu.VMEM),
         scratch_shapes=[
             pltpu.VMEM(rows_index.shape, jnp.int32),
             pltpu.VMEM(cols_index.shape, jnp.int32),
@@ -241,7 +231,8 @@
             pltpu.VMEM((tall, wide), jnp.float32),
             pltpu.VMEM((3, 3, tall, wide), jnp.float32),
             pltpu.VMEM(slots, jnp.bfloat16),
-            pltpu.SemaphoreType.DMA((5,)),
+            pltpu.VMEM(slots, jnp.bfloat16),
+            pltpu.SemaphoreType.DMA((4,)),
             pltpu.SemaphoreType.DMA((bricks,)),
             pltpu.SemaphoreType.DMA((bricks,)),
             pltpu.SemaphoreType.DMA((8,)),
@@ -253,17 +244,6 @@
             collective_id=0, has_side_effects=True, vmem_limit_bytes=60 << 20
         ),
     )(crossing, rows_index, cols_index, store, phi.reshape(points, functions))
-    strip = 64 if width % 64 == 0 else width
-    return pl.pallas_call(
-        functools.partial(gather_up, bricks),
-        out_shape=jax.ShapeDtypeStruct((own, width, width), jnp.float32),
-        grid=(width // strip,),
-        in_specs=[
-            pl.BlockSpec(memory_space=pltpu.SMEM),
-            pl.BlockSpec((bricks, strip, width), lambda i: (0, i, 0)),
-        ],
-        out_specs=pl.BlockSpec((own, strip, width), lambda i: (0, i, 0)),
-    )(crossing, landed)
 
 
 def solution(mesh):

time: 42.9 us -> 42 us (0.979)
  Pallas kernels: 42.3 us -> 39.4 us
  local copies, waits for them, and re-layouts: 0 us -> 2.06 us
    pallas_call x1 -> x0, Pallas kernels: 3.84 us -> none  [local(): pl.pallas_call(functools.partial(gather_up, bricks), out_shape=jax.ShapeD...]
    unnamed x0 -> x1, local copies, waits for them, and re-layouts: none -> 2.06 us
    pallas_call x1, Pallas kernels: 38.4 us -> 39.4 us  [local(): pl.pallas_call(functools.partial(kernel, groups, bricks, size_z), out_sha...]
where the time goes in v3:
time: 42 us; the launch traced here: 41.4 us
  Pallas kernels  39.4 us (94%)
  local copies, waits for them, and re-layouts  2.06 us (5%)
    pallas_call x1, Pallas kernels, local(): pl.pallas_call(functools.partial(kernel, groups, bricks, size_z), out_sha...  39.4 us
    unnamed x1, local copies, waits for them, and re-layouts  2.06 us

profile of v3, /device:TPU:1, one launch (start us, length us, event | category | flops | bytes accessed | tf_op | source)
XLA Modules:
  0.0 41.4 jit_solution(6285107137250665702)
XLA Ops:
  0.0 39.4 %shard_map.55 = f32[3,256,256]{2,1,0:T(8,128)} custom-call(s32[4,8]{1,0:T(4,128)} %bitcast.3, s32[1,4,256]{2,1,0:T(4,128)} %rows_hbm.1, s32[1,4,256]{2,1,0:T(4,128)} %cols_hbm.1, bf16[3,256,256]{2,1,0:T(8,128)(2,1)} %store_hbm.1, bf16[1024,1024]{1,0:T(8,128)(2,1)} %bitcast.2), custom_call_target="tpu_custom_call" | custom-call | tf_op jit(solution)/shard_map/pallas_call | solution.py:211
  39.4 2.1 %copy.7 = f32[3,256,256]{2,1,0:T(8,128)} copy(f32[3,256,256]{2,1,0:T(8,128)} %shard_map.55) | data formatting | bytes 1572864

commit v4 on v3

--- a/solution.py
+++ b/solution.py
@@ -59,14 +59,13 @@
         return lax.rem(brick + (offset % bricks), bricks)
 
     partner = functools.partial(partner_of, bricks, brick)
-    order = sorted(range(1, bricks), key=lambda r: (r == 1, r & 1, -bin(r >> 1).count("1")))
+    order = sorted(range(1, bricks), key=lambda r: (r == 1, r & 1, bin(r >> 1).count("1")))
 
     def place(dg, db):
         return (lax.rem(group + (dg % groups), groups), member(db))
 
-    around = [(dg, db) for dg in (-1, 0, 1) for db in (-1, 0, 1) if (dg, db) != (0, 0)]
     reached = {(0, r) for r in range(1, bricks)}
-    reached |= {(dg % groups, db % bricks) for dg, db in around}
+    reached |= {(1 % groups, 0), (-1 % groups, 0)}
     reached = sorted(reached)
     barrier = pltpu.get_barrier_semaphore()
     for dg, db in reached:
@@ -133,20 +132,22 @@
     for x in range(tall):
         dens[x : x + 1, :] = density[:, x * wide : (x + 1) * wide]
     halo[1, 1] = dens[...]
-    exchange = []
-    for n, (dg, db) in enumerate(around):
-        copy = pltpu.make_async_remote_copy(
-            src_ref=dens, dst_ref=halo.at[1 - dg, 1 - db],
-            send_sem=halo_send.at[n], recv_sem=halo_recv.at[n],
-            device_id=place(dg, db), device_id_type=MESH,
-        )
-        copy.start()
-        exchange.append(copy)
-    for copy in exchange:
-        copy.wait()
+    for column in (False, True):
+        exchange = []
+        for n, d in enumerate((-1, 1)):
+            copy = pltpu.make_async_remote_copy(
+                src_ref=halo.at[1] if column else dens,
+                dst_ref=halo.at[1 - d] if column else halo.at[1, 1 - d],
+                send_sem=halo_send.at[n + 2 * column], recv_sem=halo_recv.at[n + 2 * column],
+                device_id=place(0, d) if column else place(d, 0), device_id_type=MESH,
+            )
+            copy.start()
+            exchange.append(copy)
+        for copy in exchange:
+            copy.wait()
 
     field = jnp.concatenate(
-        [jnp.concatenate([halo[i, k] for k in range(3)], axis=1) for i in range(3)], axis=0
+        [jnp.concatenate([halo[k, i] for k in range(3)], axis=1) for i in range(3)], axis=0
     )
     rows, lanes = field.shape
     depth = lax.rem(lax.broadcasted_iota(jnp.int32, field.shape, 1), size_z)
@@ -235,8 +236,8 @@
             pltpu.SemaphoreType.DMA((4,)),
             pltpu.SemaphoreType.DMA((bricks,)),
             pltpu.SemaphoreType.DMA((bricks,)),
-            pltpu.SemaphoreType.DMA((8,)),
-            pltpu.SemaphoreType.DMA((8,)),
+            pltpu.SemaphoreType.DMA((4,)),
+            pltpu.SemaphoreType.DMA((4,)),
             pltpu.SemaphoreType.DMA((bricks,)),
             pltpu.SemaphoreType.DMA((bricks,)),
         ],

time: 42 us -> 43.7 us (1.040)
  Pallas kernels: 39.4 us -> 41 us
    pallas_call x1, Pallas kernels: 39.4 us -> 41 us  [local(): pl.pallas_call(functools.partial(kernel, groups, bricks, size_z), out_sha...]
where the time goes in v4:
time: 43.7 us; the launch traced here: 43.1 us
  Pallas kernels  41 us (94%)
  local copies, waits for them, and re-layouts  2.06 us (5%)
    pallas_call x1, Pallas kernels, local(): pl.pallas_call(functools.partial(kernel, groups, bricks, size_z), out_sha...  41 us
    unnamed x1, local copies, waits for them, and re-layouts  2.06 us

profile of v4, /device:TPU:1, one launch (start us, length us, event | category | flops | bytes accessed | tf_op | source)
XLA Modules:
  0.0 43.1 jit_solution(1959404927472622106)
XLA Ops:
  0.0 41.0 %shard_map.55 = f32[3,256,256]{2,1,0:T(8,128)} custom-call(s32[4,8]{1,0:T(4,128)} %bitcast.3, s32[1,4,256]{2,1,0:T(4,128)} %rows_hbm.1, s32[1,4,256]{2,1,0:T(4,128)} %cols_hbm.1, bf16[3,256,256]{2,1,0:T(8,128)(2,1)} %store_hbm.1, bf16[1024,1024]{1,0:T(8,128)(2,1)} %bitcast.2), custom_call_target="tpu_custom_call" | custom-call | tf_op jit(solution)/shard_map/pallas_call | solution.py:212
  41.1 2.1 %copy.7 = f32[3,256,256]{2,1,0:T(8,128)} copy(f32[3,256,256]{2,1,0:T(8,128)} %shard_map.55) | data formatting | bytes 1572864

commit v5 on v3

--- a/solution.py
+++ b/solution.py
@@ -59,7 +59,7 @@
         return lax.rem(brick + (offset % bricks), bricks)
 
     partner = functools.partial(partner_of, bricks, brick)
-    order = sorted(range(1, bricks), key=lambda r: (r == 1, r & 1, -bin(r >> 1).count("1")))
+    order = sorted(range(1, bricks), key=lambda r: (r == 1, r & 1, bin(r >> 1).count("1")))
 
     def place(dg, db):
         return (lax.rem(group + (dg % groups), groups), member(db))

time: 42 us -> 41.5 us (0.988)
  no operation moved by 1% of the time
where the time goes in v5:
time: 41.5 us; the launch traced here: 41.3 us
  Pallas kernels  39.2 us (94%)
  local copies, waits for them, and re-layouts  2.06 us (5%)
    pallas_call x1, Pallas kernels, local(): pl.pallas_call(functools.partial(kernel, groups, bricks, size_z), out_sha...  39.2 us
    unnamed x1, local copies, waits for them, and re-layouts  2.06 us

profile of v5, /device:TPU:1, one launch (start us, length us, event | category | flops | bytes accessed | tf_op | source)
XLA Modules:
  0.0 41.3 jit_solution(6131313598048023359)
XLA Ops:
  0.0 39.2 %shard_map.55 = f32[3,256,256]{2,1,0:T(8,128)} custom-call(s32[4,8]{1,0:T(4,128)} %bitcast.3, s32[1,4,256]{2,1,0:T(4,128)} %rows_hbm.1, s32[1,4,256]{2,1,0:T(4,128)} %cols_hbm.1, bf16[3,256,256]{2,1,0:T(8,128)(2,1)} %store_hbm.1, bf16[1024,1024]{1,0:T(8,128)(2,1)} %bitcast.2), custom_call_target="tpu_custom_call" | custom-call | tf_op jit(solution)/shard_map/pallas_call | solution.py:211
  39.2 2.1 %copy.7 = f32[3,256,256]{2,1,0:T(8,128)} copy(f32[3,256,256]{2,1,0:T(8,128)} %shard_map.55) | data formatting | bytes 1572864
